TPU v7x, 256 devices: a whole 4x4x8 slice. The times are simulated.
256 devices in a mesh: gz: 4 (over z_lo, core), xy: 64 (over y, x, z_hi).
Axes of the slice: x: 4, y: 4, z: 8 (z_hi: 4, z_lo: 2; z = z_hi * 2 + z_lo), core: 2. Of those that a mesh axis runs over, the one named last changes fastest.
Arguments:
- features: float32 [64, 128, 28, 256], P('gz', 'xy'), may hold values from -6 to 6
- block_mask: int32 [32, 64, 14], P('gz', 'xy'), may hold values 0 or 1
- near_kernel_weight: float32 [27, 256, 256], P(None, None, 'xy'), may hold values from -0.078125 to 0.078125
- far_kernel_weight: float32 [27, 256, 256], P(None, None, 'xy'), may hold values from -0.078125 to 0.078125
Outputs:
- section_out: float32 [64, 128, 28, 256], P('gz', 'xy')
All inputs are finite; a program needn't handle non-finite values. No bound on the sum of `block_mask` on one device may be relied on, other than what follows from the above.
Results may differ from a plain program's by a relative error of at most 0.00005.
Values sent between devices are 32-bit elements; how exact they have to be, the bound alone decides.
No kernel may reach another device: no remote copies, remote signals or barrier semaphores. Data moves between devices by JAX's collectives and lax.ppermute only.
A program may use at most 128 MiB of HBM per device.

v0:
```python
import jax
import jax.numpy as jnp
from jax import lax
from jax.sharding import PartitionSpec as P

B = 2
NEAR_DILATION = 16
FAR_DILATION = 32


def from_behind(block, axis, distance):
    devices = range(lax.axis_size(axis))
    route = [(i - distance, i) for i in devices if i - distance in devices]
    return lax.ppermute(block, axis, route)


def stack_z(field, step):
    lower = from_behind(field, "gz", step)
    upper = from_behind(field, "gz", -step)
    return jnp.stack((lower, field, upper), 0)


def stack_x(field, step):
    lower = from_behind(field, "xy", step)
    upper = from_behind(field, "xy", -step)
    return jnp.stack((lower, field, upper), 0)


def neighbours(field, step_z, step_x):
    both = stack_x(stack_z(field, step_z), step_x)
    return [[both[col, row] for col in range(3)] for row in range(3)]


def dilated_result(field, weight, dilation):
    slab_z, slab_x, span_y, channels = field.shape
    grid = neighbours(field, dilation // slab_z, dilation // slab_x)
    windows = []
    for row in range(3):
        for col in range(3):
            padded = jnp.pad(grid[row][col], ((0, 0), (0, 0), (dilation, dilation), (0, 0)))
            for lane in range(3):
                windows.append(padded[:, :, lane * dilation : lane * dilation + span_y, :])
    columns = jnp.concatenate(windows, 3).reshape(slab_z * slab_x * span_y, 27 * channels)
    summed = jnp.dot(
        columns,
        weight.reshape(27 * channels, weight.shape[2]),
        precision=lax.Precision.HIGHEST,
        preferred_element_type=jnp.float32,
    )
    return summed.reshape(slab_z, slab_x, span_y, weight.shape[2])


def local(features, block_mask, near_kernel_weight, far_kernel_weight):
    active_blocks = jnp.repeat(jnp.repeat(jnp.repeat(block_mask, B, 0), B, 1), B, 2)
    active_blocks = active_blocks.astype(jnp.float32)[..., None]
    dense_near_output = lax.all_gather(near_kernel_weight, "xy", axis=2, tiled=True)
    masked_input = active_blocks * features
    hidden_state = active_blocks * jnp.maximum(
        dilated_result(masked_input, dense_near_output, NEAR_DILATION), 0.0
    )
    dense_far_output = lax.all_gather(far_kernel_weight, "xy", axis=2, tiled=True)
    return active_blocks * (
        masked_input + dilated_result(hidden_state, dense_far_output, FAR_DILATION)
    )


def solution(mesh):
    in_specs = (
        P("gz", "xy", None, None),
        P("gz", "xy", None),
        P(None, None, "xy"),
        P(None, None, "xy"),
    )
    out_specs = P("gz", "xy", None, None)
    return jax.shard_map(local, mesh=mesh, in_specs=in_specs, out_specs=out_specs, check_vma=False)
```

profile of v0, /device:TPU:10, one launch (start us, length us, event | category | flops | bytes accessed | tf_op | source)
XLA Modules:
  0.0 468.5 jit_solution(18436965677184561776)
XLA Ops:
  6.5 1.6 copy.36
  9.1 1.4 fusion.29
  11.0 1.3 collective-permute-start.1
  12.3 3.1 collective-permute-start
  15.4 1.6 copy.46
  17.0 1.7 copy.70
  20.2 1.6 copy.32
  21.8 4.0 collective-permute-start.2
  25.9 4.2 collective-permute-start.3
  30.5 52.4 %collective-permute-done.2 = f32[3,16,2,28,256]{4,1,3,2,0:T(8,128)S(1)} collective-permute-done((f32[3,16,2,28,256]{4,1,3,2,0:T(8,128)S(1)}, f32[3,16,2,28,256]{4,1,3,2,0:T(8,128)S(1)}, u32[]{:S(2)}, u32[]{:S(2)}) %collective-permute-start.2) | collective-permute-done | bytes 2752544 | tf_op jit(solution)/shard_map/ppermute | solution.py:14
  82.9 1.6 copy.67
  84.5 57.5 %collective-permute-done.3 = f32[3,16,2,28,256]{4,1,3,2,0:T(8,128)S(1)} collective-permute-done((f32[3,16,2,28,256]{4,1,3,2,0:T(8,128)S(1)}, f32[3,16,2,28,256]{4,1,3,2,0:T(8,128)S(1)}, u32[]{:S(2)}, u32[]{:S(2)}) %collective-permute-start.3) | collective-permute-done | bytes 2752544 | tf_op jit(solution)/shard_map/ppermute | solution.py:14
  142.0 1.6 copy.66
  145.2 1.2 constant_dynamic-update-slice_fusion.8
  148.6 1.2 constant_dynamic-update-slice_fusion.7
  151.3 1.2 fusion.6
  153.6 1.2 fusion.7
  160.4 1.2 fusion.11
  163.9 1.2 fusion.13
  165.1 1.2 fusion.14
  167.5 1.2 fusion.15
  171.0 1.2 fusion.17
  172.2 1.2 fusion.18
  174.5 1.2 fusion.19
  175.7 56.7 %all-gather.3.cloned.1.call-done = f32[27,256,256]{1,0,2:T(8,128)} async-done(((f32[27,256,4]{1,0,2:T(8,128)}), f32[27,256,256]{1,0,2:T(8,128)}) %all-gather.3.cloned.1.call-update) | async-done | bytes 7077904 | tf_op jit(solution)/shard_map/all_gather | solution.py:56
  232.3 10.1 %copy.37 = f32[27,256,256]{2,1,0:T(8,128)} copy(f32[27,256,256]{1,0,2:T(8,128)} %all-gather.3.cloned.1.call-done) | data formatting | bytes 14155776 | tf_op jit(solution)/shard_map/all_gather | solution.py:56
  242.5 27.0 %fusion = f32[16,2,28,256]{3,2,1,0:T(8,128)S(1)} fusion(f32[16,2,28,6912]{3,2,1,0:T(8,128)} %fusion.19, f32[6912,256,1,1]{1,0,3,2:T(8,128)} %bitcast.134, f32[16,28]{1,0:T(8,128)S(1)} %copy.26), kind=kOutput, calls=%fused_computation.25 | convolution fusion | flops 19025821696 | bytes 32769792 | tf_op jit(solution)/shard_map/dot_general | solution.py:44
  270.0 1.3 collective-permute-start.5
  271.3 10.9 %collective-permute-start.4 = (f32[16,2,28,256]{3,0,2,1:T(8,128)S(1)}, f32[16,2,28,256]{3,0,2,1:T(8,128)S(1)}, u32[]{:S(2)}, u32[]{:S(2)}) collective-permute-start(f32[16,2,28,256]{3,0,2,1:T(8,128)S(1)} %copy.38), channel_id=1, source_target_pairs={{0,128},{64,192},{1,129},{65,193},{2,130},{66,194},{3,131},{67,195... | collective-permute-start | bytes 2752520 | tf_op jit(solution)/shard_map/ppermute | solution.py:14
  282.2 31.5 %collective-permute-done.5 = f32[16,2,28,256]{3,0,2,1:T(8,128)S(1)} collective-permute-done((f32[16,2,28,256]{3,0,2,1:T(8,128)S(1)}, f32[16,2,28,256]{3,0,2,1:T(8,128)S(1)}, u32[]{:S(2)}, u32[]{:S(2)}) %collective-permute-start.5) | collective-permute-done | bytes 917536 | tf_op jit(solution)/shard_map/ppermute | solution.py:14
  315.5 3.1 copy.42
  318.6 3.4 collective-permute-start.6
  322.0 3.9 collective-permute-start.7
  327.1 35.3 %all-gather.5.cloned.1.call-done = f32[27,256,256]{1,0,2:T(8,128)} async-done(((f32[27,256,4]{1,0,2:T(8,128)}), f32[27,256,256]{1,0,2:T(8,128)}) %all-gather.5.cloned.1.call-update) | async-done | bytes 7077904 | tf_op jit(solution)/shard_map/all_gather | solution.py:61
  362.4 9.7 %copy.47 = f32[27,256,256]{2,1,0:T(8,128)} copy(f32[27,256,256]{1,0,2:T(8,128)} %all-gather.5.cloned.1.call-done) | data formatting | bytes 14155776 | tf_op jit(solution)/shard_map/all_gather | solution.py:61
  372.1 23.5 %collective-permute-done.6 = f32[3,16,2,28,256]{4,1,3,2,0:T(8,128)} collective-permute-done((f32[3,16,2,28,256]{4,1,3,2,0:T(8,128)}, f32[3,16,2,28,256]{4,1,3,2,0:T(8,128)}, u32[]{:S(2)}, u32[]{:S(2)}) %collective-permute-start.6) | collective-permute-done | bytes 2752544 | tf_op jit(solution)/shard_map/ppermute | solution.py:14
  395.6 3.4 copy.65
  399.0 1.2 fusion.28
  405.8 3.4 copy.64
  409.2 1.2 fusion.26
  417.1 1.2 broadcast_dynamic-update-slice_fusion.7
  420.6 1.2 broadcast_dynamic-update-slice_fusion.5
  421.8 1.2 broadcast_dynamic-update-slice_fusion.4
  424.1 1.2 broadcast_dynamic-update-slice_fusion.3
  427.6 1.2 broadcast_dynamic-update-slice_fusion.1
  431.0 1.2 broadcast_dynamic-update-slice_fusion.17
  432.3 27.5 %fusion.1 = f32[16,2,28,256]{3,2,1,0:T(8,128)S(1)} fusion(f32[16,2,28,6912]{3,2,1,0:T(8,128)} %broadcast_dynamic-update-slice_fusion.17, f32[6912,256,1,1]{1,0,3,2:T(8,128)S(1)} %bitcast.125, f32[16,28]{1,0:T(8,128)S(1)} %copy.26, f32[16,2,28,256]{3,1,2,0:T(2,128)S(1)} %copy-done), kind=kOutput, calls=%fused_computation.27 | convolution fusion | flops 19026051072 | bytes 33687296 | tf_op jit(solution)/shard_map/dot_general | solution.py:44
  459.8 1.6 copy.48
  (66 shorter events, 46.0 us)
Async XLA Ops:
  6.5 225.8 %all-gather.3.cloned.1.call-start = ((), (), s32[]{:S(2)}) async-start(), calls=%async_computation | async-start | bytes 8519680 | tf_op jit(solution)/shard_map/all_gather | solution.py:56
  8.1 354.3 %all-gather.5.cloned.1.call-start = ((), (), s32[]{:S(2)}) async-start(), calls=%async_computation.1 | async-start | bytes 8519680 | tf_op jit(solution)/shard_map/all_gather | solution.py:61
  11.0 6.0 %collective-permute-start.1 = (f32[16,2,28,256]{3,0,2,1:T(8,128)S(1)}, f32[16,2,28,256]{3,0,2,1:T(8,128)}, u32[]{:S(2)}, u32[]{:S(2)}) collective-permute-start(f32[16,2,28,256]{3,0,2,1:T(8,128)S(1)} %copy.28), channel_id=1, source_target_pairs={{64,0},{128,64},{192,128},{65,1},{129,65},{193,129},{66,2},{130,66... | collective-permute-start | bytes 2752520 | tf_op jit(solution)/shard_map/ppermute | solution.py:14
  12.3 6.4 %collective-permute-start = (f32[16,2,28,256]{3,0,2,1:T(8,128)S(1)}, f32[16,2,28,256]{3,0,2,1:T(8,128)S(1)}, u32[]{:S(2)}, u32[]{:S(2)}) collective-permute-start(f32[16,2,28,256]{3,0,2,1:T(8,128)S(1)} %copy.28), channel_id=1, source_target_pairs={{0,64},{64,128},{128,192},{1,65},{65,129},{129,193},{2,66},{66,130... | collective-permute-start | bytes 2752520 | tf_op jit(solution)/shard_map/ppermute | solution.py:14
  21.8 61.1 %collective-permute-start.2 = (f32[3,16,2,28,256]{4,1,3,2,0:T(8,128)S(1)}, f32[3,16,2,28,256]{4,1,3,2,0:T(8,128)S(1)}, u32[]{:S(2)}, u32[]{:S(2)}) collective-permute-start(f32[3,16,2,28,256]{4,1,3,2,0:T(8,128)S(1)} %copy.32), channel_id=1, source_target_pairs={{0,8},{1,9},{2,10},{3,11},{4,12},{5,13},{6,14},{7,15},{8,16},{9,17... | collective-permute-start | bytes 8257544 | tf_op jit(solution)/shard_map/ppermute | solution.py:14
  25.9 116.1 %collective-permute-start.3 = (f32[3,16,2,28,256]{4,1,3,2,0:T(8,128)S(1)}, f32[3,16,2,28,256]{4,1,3,2,0:T(8,128)S(1)}, u32[]{:S(2)}, u32[]{:S(2)}) collective-permute-start(f32[3,16,2,28,256]{4,1,3,2,0:T(8,128)S(1)} %copy.32), channel_id=1, source_target_pairs={{8,0},{9,1},{10,2},{11,3},{12,4},{13,5},{14,6},{15,7},{16,8},{17,9... | collective-permute-start | bytes 8257544 | tf_op jit(solution)/shard_map/ppermute | solution.py:14
  270.0 43.7 %collective-permute-start.5 = (f32[16,2,28,256]{3,0,2,1:T(8,128)S(1)}, f32[16,2,28,256]{3,0,2,1:T(8,128)S(1)}, u32[]{:S(2)}, u32[]{:S(2)}) collective-permute-start(f32[16,2,28,256]{3,0,2,1:T(8,128)S(1)} %copy.38), channel_id=1, source_target_pairs={{128,0},{192,64},{129,1},{193,65},{130,2},{194,66},{131,3},{195,67... | collective-permute-start | bytes 2752520 | tf_op jit(solution)/shard_map/ppermute | solution.py:14
  271.3 42.9 %collective-permute-start.4 = (f32[16,2,28,256]{3,0,2,1:T(8,128)S(1)}, f32[16,2,28,256]{3,0,2,1:T(8,128)S(1)}, u32[]{:S(2)}, u32[]{:S(2)}) collective-permute-start(f32[16,2,28,256]{3,0,2,1:T(8,128)S(1)} %copy.38), channel_id=1, source_target_pairs={{0,128},{64,192},{1,129},{65,193},{2,130},{66,194},{3,131},{67,195... | collective-permute-start | bytes 2752520 | tf_op jit(solution)/shard_map/ppermute | solution.py:14
  318.6 76.9 %collective-permute-start.6 = (f32[3,16,2,28,256]{4,1,3,2,0:T(8,128)}, f32[3,16,2,28,256]{4,1,3,2,0:T(8,128)}, u32[]{:S(2)}, u32[]{:S(2)}) collective-permute-start(f32[3,16,2,28,256]{4,1,3,2,0:T(8,128)} %copy.42), channel_id=1, source_target_pairs={{0,16},{1,17},{2,18},{3,19},{4,20},{5,21},{6,22},{7,23},{8,24},{9,... | collective-permute-start | bytes 8257544 | tf_op jit(solution)/shard_map/ppermute | solution.py:14
  322.0 83.8 %collective-permute-start.7 = (f32[3,16,2,28,256]{4,1,3,2,0:T(8,128)}, f32[3,16,2,28,256]{4,1,3,2,0:T(8,128)}, u32[]{:S(2)}, u32[]{:S(2)}) collective-permute-start(f32[3,16,2,28,256]{4,1,3,2,0:T(8,128)} %copy.42), channel_id=1, source_target_pairs={{16,0},{17,1},{18,2},{19,3},{20,4},{21,5},{22,6},{23,7},{24,8},{25... | collective-permute-start | bytes 8257544 | tf_op jit(solution)/shard_map/ppermute | solution.py:14
  372.1 60.1 %slice-start = ((s8[7077888]{0:T(1024)(128)(4,1)}), s8[4194304]{0:T(1024)(128)(4,1)S(1)}, s32[]{:S(2)}) async-start(s8[7077888]{0:T(1024)(128)(4,1)} %bitcast.123), calls=%async_computation.2 | async-start | bytes 8388608
  372.1 60.1 %copy-start = (f32[16,2,28,256]{3,1,2,0:T(2,128)S(1)}, f32[16,2,28,256]{3,1,2,0:T(2,128)}, u32[]{:S(2)}) copy-start(f32[16,2,28,256]{3,1,2,0:T(2,128)} %param.4) | copy-start | bytes 2752516
  411.5 20.7 %slice-start.1 = ((s8[7077888]{0:T(1024)(128)(4,1)}), s8[2883584]{0:T(1024)(128)(4,1)S(1)}, s32[]{:S(2)}) async-start(s8[7077888]{0:T(1024)(128)(4,1)} %bitcast.123), calls=%async_computation.3 | async-start | bytes 5767168
Sparse Core Ops, SparseCore 0:
  10.6 221.6 all-gather.2
  235.6 126.7 all-gather.4
where the time goes:
time: 478 us; the launch traced here: 468 us
  waiting for transfers between devices  257 us (54%)
  local copies, waits for them, and re-layouts  107 us (22%)
  matrix products  54.5 us (11%)
  starting transfers between devices  32.2 us (7%)
  between operations  13.9 us (3%)
    ppermute x8, waiting for transfers between devices, from_behind(): return lax.ppermute(block, axis, route)  165 us
    unnamed x60, local copies, waits for them, and re-layouts  63 us
    all_gather x1, waiting for transfers between devices, local(): lax.all_gather(near_kernel_weight, 'xy', axis=2, tiled=True)  56.7 us
    dot_general x2, matrix products, dilated_result(): jnp.dot(columns, weight.reshape(27 * channels, weight.shape[2]), precisio...  54.5 us
    all_gather x1, waiting for transfers between devices, local(): lax.all_gather(far_kernel_weight, 'xy', axis=2, tiled=True)  35.3 us
    ppermute x8, starting transfers between devices, from_behind(): return lax.ppermute(block, axis, route)  32.1 us
    ppermute x8, local copies, waits for them, and re-layouts, from_behind(): return lax.ppermute(block, axis, route)  13.3 us
    all_gather x1, local copies, waits for them, and re-layouts, local(): lax.all_gather(near_kernel_weight, 'xy', axis=2, tiled=True)  10.1 us
  transfers between devices with their start and end apart: 10, of which 6 were waited for; matrix products, arithmetic and copies ran while one was open for 23% of the time, Pallas kernels for 0%

commit v1 on v0

--- a/solution.py
+++ b/solution.py
@@ -6,6 +6,12 @@
 B = 2
 NEAR_DILATION = 16
 FAR_DILATION = 32
+
+
+def manage_tasks_in(local_x):
+    s_next = jnp.stack([local_x for _ in range(jax.lax.axis_size("xy"))])
+    mat_out = jax.lax.all_to_all(s_next, "xy", 0, 0)
+    return jnp.concatenate(mat_out, axis=2)
 
 
 def from_behind(block, axis, distance):
@@ -53,7 +59,7 @@
 def local(features, block_mask, near_kernel_weight, far_kernel_weight):
     active_blocks = jnp.repeat(jnp.repeat(jnp.repeat(block_mask, B, 0), B, 1), B, 2)
     active_blocks = active_blocks.astype(jnp.float32)[..., None]
-    dense_near_output = lax.all_gather(near_kernel_weight, "xy", axis=2, tiled=True)
+    dense_near_output = manage_tasks_in(near_kernel_weight)
     masked_input = active_blocks * features
     hidden_state = active_blocks * jnp.maximum(
         dilated_result(masked_input, dense_near_output, NEAR_DILATION), 0.0

time: 478 us -> 541 us (1.13)
  starting transfers between devices: 32.2 us -> 170 us
  waiting for transfers between devices: 257 us -> 179 us
    ppermute x8, starting transfers between devices: 32.1 us -> 155 us  [from_behind(): return lax.ppermute(block, axis, route)]
    all_gather x1 -> x0, waiting for transfers between devices: 56.7 us -> none  [local(): lax.all_gather(near_kernel_weight, 'xy', axis=2, tiled=True)]
    all_gather x1, waiting for transfers between devices: 35.3 us -> 0.01 us  [local(): lax.all_gather(far_kernel_weight, 'xy', axis=2, tiled=True)]
    all_to_all x0 -> x1, starting transfers between devices: none -> 14.7 us  [manage_tasks_in(): mat_out = jax.lax.all_to_all(s_next, 'xy', 0, 0)]
    ppermute x8, waiting for transfers between devices: 165 us -> 179 us  [from_behind(): return lax.ppermute(block, axis, route)]
    all_gather x1 -> x0, local copies, waits for them, and re-layouts: 10.1 us -> none  [local(): lax.all_gather(near_kernel_weight, 'xy', axis=2, tiled=True)]
  transfers between devices with their start and end apart: 10 -> 10, of which waited for: 6 -> 5; matrix products, arithmetic and copies ran while one was open for 23% -> 21% of each run, Pallas kernels for 0% -> 0%
where the time goes in v1:
time: 541 us; the launch traced here: 533 us
  waiting for transfers between devices  179 us (33%)
  starting transfers between devices  170 us (31%)
  local copies, waits for them, and re-layouts  112 us (21%)
  matrix products  54.6 us (10%)
  between operations  13.8 us (3%)
    ppermute x8, waiting for transfers between devices, from_behind(): return lax.ppermute(block, axis, route)  179 us
    ppermute x8, starting transfers between devices, from_behind(): return lax.ppermute(block, axis, route)  155 us
    unnamed x60, local copies, waits for them, and re-layouts  68.3 us
    dot_general x2, matrix products, dilated_result(): jnp.dot(columns, weight.reshape(27 * channels, weight.shape[2]), precisio...  54.6 us
    all_to_all x1, starting transfers between devices, manage_tasks_in(): mat_out = jax.lax.all_to_all(s_next, 'xy', 0, 0)  14.7 us
    ppermute x8, local copies, waits for them, and re-layouts, from_behind(): return lax.ppermute(block, axis, route)  13.3 us
  transfers between devices with their start and end apart: 10, of which 5 were waited for; matrix products, arithmetic and copies ran while one was open for 21% of the time, Pallas kernels for 0%

profile of v1, /device:TPU:10, one launch (start us, length us, event | category | flops | bytes accessed | tf_op | source)
XLA Modules:
  0.0 532.5 jit_solution(3817843006018019465)
XLA Ops:
  6.5 4.7 stack.37
  11.2 14.7 %all-to-all-start = ((f32[64,27,256,4]{2,3,1,0:T(4,128)}), f32[64,27,256,4]{2,3,1,0:T(4,128)}, u32[]{:S(2)}, u32[]{:S(2)}) async-start(f32[64,27,256,4]{2,3,1,0:T(4,128)} %stack.37), calls=%async_computation | async-start | bytes 14155776 | tf_op jit(solution)/shard_map/all_to_all | solution.py:13
  26.9 1.4 fusion.36
  28.8 1.3 collective-permute-start.1
  30.1 3.1 collective-permute-start
  33.2 1.6 copy.48
  34.9 1.7 copy.74
  38.1 1.6 copy.34
  39.6 4.0 collective-permute-start.2
  43.7 4.4 collective-permute-start.3
  48.5 62.1 %collective-permute-done.2 = f32[3,16,2,28,256]{4,1,3,2,0:T(8,128)S(1)} collective-permute-done((f32[3,16,2,28,256]{4,1,3,2,0:T(8,128)S(1)}, f32[3,16,2,28,256]{4,1,3,2,0:T(8,128)S(1)}, u32[]{:S(2)}, u32[]{:S(2)}) %collective-permute-start.2) | collective-permute-done | bytes 2752544 | tf_op jit(solution)/shard_map/ppermute | solution.py:20
  110.5 1.6 copy.71
  112.1 52.0 %collective-permute-done.3 = f32[3,16,2,28,256]{4,1,3,2,0:T(8,128)S(1)} collective-permute-done((f32[3,16,2,28,256]{4,1,3,2,0:T(8,128)S(1)}, f32[3,16,2,28,256]{4,1,3,2,0:T(8,128)S(1)}, u32[]{:S(2)}, u32[]{:S(2)}) %collective-permute-start.3) | collective-permute-done | bytes 2752544 | tf_op jit(solution)/shard_map/ppermute | solution.py:20
  164.2 1.6 copy.70
  167.3 1.2 constant_dynamic-update-slice_fusion.8
  169.6 1.2 fusion.11
  173.5 1.2 fusion.13
  176.9 1.2 fusion.15
  184.9 1.2 constant_dynamic-update-slice_fusion.3
  187.2 1.2 fusion.21
  188.4 1.2 constant_dynamic-update-slice_fusion.2
  189.6 1.2 fusion.22
  192.0 1.2 constant_dynamic-update-slice_fusion.1
  194.3 1.2 fusion.25
  195.5 1.2 constant_dynamic-update-slice_fusion
  196.7 1.2 fusion.26
  197.8 4.7 copy.38
  202.6 6.7 %copy.54 = f32[32,8,27,256]{3,1,2,0:T(8,128)S(1)} copy(f32[32,8,27,256]{3,2,1,0:T(8,128)S(1)} %bitcast.130) | data formatting | bytes 14155776
  209.3 27.1 %fusion.5 = f32[16,2,28,256]{3,2,1,0:T(8,128)S(1)} fusion(f32[16,2,28,6912]{3,2,1,0:T(8,128)} %fusion.26, f32[6912,256]{0,1:T(8,128)S(1)} %bitcast.142, f32[16,28]{1,0:T(8,128)S(1)} %copy.28), kind=kOutput, calls=%fused_computation.27 | convolution fusion | flops 19025821696 | bytes 32769792 | tf_op jit(solution)/shard_map/dot_general | solution.py:50
  237.0 1.3 collective-permute-start.5
  238.3 133.5 %collective-permute-start.4 = (f32[16,2,28,256]{3,0,2,1:T(8,128)S(1)}, f32[16,2,28,256]{3,0,2,1:T(8,128)S(1)}, u32[]{:S(2)}, u32[]{:S(2)}) collective-permute-start(f32[16,2,28,256]{3,0,2,1:T(8,128)S(1)} %copy.40), channel_id=1, source_target_pairs={{0,128},{64,192},{1,129},{65,193},{2,130},{66,194},{3,131},{67,195... | collective-permute-start | bytes 2752520 | tf_op jit(solution)/shard_map/ppermute | solution.py:20
  371.7 18.7 %collective-permute-done.5 = f32[16,2,28,256]{3,0,2,1:T(8,128)S(1)} collective-permute-done((f32[16,2,28,256]{3,0,2,1:T(8,128)S(1)}, f32[16,2,28,256]{3,0,2,1:T(8,128)S(1)}, u32[]{:S(2)}, u32[]{:S(2)}) %collective-permute-start.5) | collective-permute-done | bytes 917536 | tf_op jit(solution)/shard_map/ppermute | solution.py:20
  392.9 3.1 copy.44
  396.1 3.4 collective-permute-start.6
  399.5 3.9 collective-permute-start.7
  404.5 9.7 %copy.49 = f32[27,256,256]{2,1,0:T(8,128)} copy(f32[27,256,256]{1,0,2:T(8,128)} %all-gather.2.cloned.1.call-done) | data formatting | bytes 14155776 | tf_op jit(solution)/shard_map/all_gather | solution.py:67
  414.2 45.4 %collective-permute-done.6 = f32[3,16,2,28,256]{4,1,3,2,0:T(8,128)} collective-permute-done((f32[3,16,2,28,256]{4,1,3,2,0:T(8,128)}, f32[3,16,2,28,256]{4,1,3,2,0:T(8,128)}, u32[]{:S(2)}, u32[]{:S(2)}) %collective-permute-start.6) | collective-permute-done | bytes 2752544 | tf_op jit(solution)/shard_map/ppermute | solution.py:20
  459.6 3.4 copy.69
  463.0 1.2 fusion.35
  465.4 1.2 broadcast_dynamic-update-slice_fusion.14
  468.8 1.2 broadcast_dynamic-update-slice_fusion.12
  469.9 3.4 copy.68
  483.5 1.2 fusion.30
  487.0 1.2 fusion.29
  488.2 1.2 broadcast_dynamic-update-slice_fusion.3
  493.9 1.2 fusion.27
  496.3 27.5 %fusion.8 = f32[16,2,28,256]{3,2,1,0:T(8,128)S(1)} fusion(f32[16,2,28,6912]{3,2,1,0:T(8,128)} %broadcast_dynamic-update-slice_fusion.17, f32[6912,256,1,1]{1,0,3,2:T(8,128)S(1)} %bitcast.133, f32[16,28]{1,0:T(8,128)S(1)} %copy.28, f32[16,2,28,256]{3,1,2,0:T(2,128)S(1)} %copy-done), kind=kOutput, calls=%fused_computation.29 | convolution fusion | flops 19026051072 | bytes 33687296 | tf_op jit(solution)/shard_map/dot_general | solution.py:50
  523.9 1.6 copy.50
  (66 shorter events, 46.8 us)
Async XLA Ops:
  11.2 186.6 %all-to-all-start = ((f32[64,27,256,4]{2,3,1,0:T(4,128)}), f32[64,27,256,4]{2,3,1,0:T(4,128)}, u32[]{:S(2)}, u32[]{:S(2)}) async-start(f32[64,27,256,4]{2,3,1,0:T(4,128)} %stack.37), calls=%async_computation | async-start | bytes 14155776 | tf_op jit(solution)/shard_map/all_to_all | solution.py:13
  25.9 378.6 %all-gather.2.cloned.1.call-start = ((), (), s32[]{:S(2)}) async-start(), calls=%async_computation.1 | async-start | bytes 8519680 | tf_op jit(solution)/shard_map/all_gather | solution.py:67
  28.8 6.0 %collective-permute-start.1 = (f32[16,2,28,256]{3,0,2,1:T(8,128)S(1)}, f32[16,2,28,256]{3,0,2,1:T(8,128)}, u32[]{:S(2)}, u32[]{:S(2)}) collective-permute-start(f32[16,2,28,256]{3,0,2,1:T(8,128)S(1)} %copy.30), channel_id=1, source_target_pairs={{64,0},{128,64},{192,128},{65,1},{129,65},{193,129},{66,2},{130,66... | collective-permute-start | bytes 2752520 | tf_op jit(solution)/shard_map/ppermute | solution.py:20
  30.1 6.4 %collective-permute-start = (f32[16,2,28,256]{3,0,2,1:T(8,128)S(1)}, f32[16,2,28,256]{3,0,2,1:T(8,128)S(1)}, u32[]{:S(2)}, u32[]{:S(2)}) collective-permute-start(f32[16,2,28,256]{3,0,2,1:T(8,128)S(1)} %copy.30), channel_id=1, source_target_pairs={{0,64},{64,128},{128,192},{1,65},{65,129},{129,193},{2,66},{66,130... | collective-permute-start | bytes 2752520 | tf_op jit(solution)/shard_map/ppermute | solution.py:20
  39.6 70.9 %collective-permute-start.2 = (f32[3,16,2,28,256]{4,1,3,2,0:T(8,128)S(1)}, f32[3,16,2,28,256]{4,1,3,2,0:T(8,128)S(1)}, u32[]{:S(2)}, u32[]{:S(2)}) collective-permute-start(f32[3,16,2,28,256]{4,1,3,2,0:T(8,128)S(1)} %copy.34), channel_id=1, source_target_pairs={{0,8},{1,9},{2,10},{3,11},{4,12},{5,13},{6,14},{7,15},{8,16},{9,17... | collective-permute-start | bytes 8257544 | tf_op jit(solution)/shard_map/ppermute | solution.py:20
  43.7 120.5 %collective-permute-start.3 = (f32[3,16,2,28,256]{4,1,3,2,0:T(8,128)S(1)}, f32[3,16,2,28,256]{4,1,3,2,0:T(8,128)S(1)}, u32[]{:S(2)}, u32[]{:S(2)}) collective-permute-start(f32[3,16,2,28,256]{4,1,3,2,0:T(8,128)S(1)} %copy.34), channel_id=1, source_target_pairs={{8,0},{9,1},{10,2},{11,3},{12,4},{13,5},{14,6},{15,7},{16,8},{17,9... | collective-permute-start | bytes 8257544 | tf_op jit(solution)/shard_map/ppermute | solution.py:20
  237.0 153.5 %collective-permute-start.5 = (f32[16,2,28,256]{3,0,2,1:T(8,128)S(1)}, f32[16,2,28,256]{3,0,2,1:T(8,128)S(1)}, u32[]{:S(2)}, u32[]{:S(2)}) collective-permute-start(f32[16,2,28,256]{3,0,2,1:T(8,128)S(1)} %copy.40), channel_id=1, source_target_pairs={{128,0},{192,64},{129,1},{193,65},{130,2},{194,66},{131,3},{195,67... | collective-permute-start | bytes 2752520 | tf_op jit(solution)/shard_map/ppermute | solution.py:20
  238.3 153.4 %collective-permute-start.4 = (f32[16,2,28,256]{3,0,2,1:T(8,128)S(1)}, f32[16,2,28,256]{3,0,2,1:T(8,128)S(1)}, u32[]{:S(2)}, u32[]{:S(2)}) collective-permute-start(f32[16,2,28,256]{3,0,2,1:T(8,128)S(1)} %copy.40), channel_id=1, source_target_pairs={{0,128},{64,192},{1,129},{65,193},{2,130},{66,194},{3,131},{67,195... | collective-permute-start | bytes 2752520 | tf_op jit(solution)/shard_map/ppermute | solution.py:20
  396.1 63.5 %collective-permute-start.6 = (f32[3,16,2,28,256]{4,1,3,2,0:T(8,128)}, f32[3,16,2,28,256]{4,1,3,2,0:T(8,128)}, u32[]{:S(2)}, u32[]{:S(2)}) collective-permute-start(f32[3,16,2,28,256]{4,1,3,2,0:T(8,128)} %copy.44), channel_id=1, source_target_pairs={{0,16},{1,17},{2,18},{3,19},{4,20},{5,21},{6,22},{7,23},{8,24},{9,... | collective-permute-start | bytes 8257544 | tf_op jit(solution)/shard_map/ppermute | solution.py:20
  399.5 70.5 %collective-permute-start.7 = (f32[3,16,2,28,256]{4,1,3,2,0:T(8,128)}, f32[3,16,2,28,256]{4,1,3,2,0:T(8,128)}, u32[]{:S(2)}, u32[]{:S(2)}) collective-permute-start(f32[3,16,2,28,256]{4,1,3,2,0:T(8,128)} %copy.44), channel_id=1, source_target_pairs={{16,0},{17,1},{18,2},{19,3},{20,4},{21,5},{22,6},{23,7},{24,8},{25... | collective-permute-start | bytes 8257544 | tf_op jit(solution)/shard_map/ppermute | solution.py:20
  414.2 82.1 %slice-start = ((s8[7077888]{0:T(1024)(128)(4,1)}), s8[4194304]{0:T(1024)(128)(4,1)S(1)}, s32[]{:S(2)}) async-start(s8[7077888]{0:T(1024)(128)(4,1)} %bitcast.131), calls=%async_computation.2 | async-start | bytes 8388608
  414.2 82.1 %copy-start = (f32[16,2,28,256]{3,1,2,0:T(2,128)S(1)}, f32[16,2,28,256]{3,1,2,0:T(2,128)}, u32[]{:S(2)}) copy-start(f32[16,2,28,256]{3,1,2,0:T(2,128)} %param.4) | copy-start | bytes 2752516
  475.6 20.7 %slice-start.1 = ((s8[7077888]{0:T(1024)(128)(4,1)}), s8[2883584]{0:T(1024)(128)(4,1)S(1)}, s32[]{:S(2)}) async-start(s8[7077888]{0:T(1024)(128)(4,1)} %bitcast.131), calls=%async_computation.3 | async-start | bytes 5767168
Sparse Core Ops, SparseCore 0:
  35.0 218.0 all-gather.1
